TPU v7x, 32 devices: a whole 2x2x4 slice. The times are simulated.
32 devices in a mesh: grp: 2 (over y), smp: 4 (over x, core), row: 4 (over z).
Axes of the slice: x: 2, y: 2, z: 4, core: 2. Of those that a mesh axis runs over, the one named last changes fastest.
Arguments:
- positions: float32 [8, 3, 4096], P(('grp', 'smp'), None, 'row'), parts along dimension 0, may hold values from -60 to 60
- noise_draw: float32 [8, 3, 4096], P(('grp', 'smp'), None, 'row'), parts along dimension 0, may hold values from -6 to 6
- noise_level: float32 [8], P(('grp', 'smp')), parts along dimension 0, may hold values from 0.5 to 80
- atom_single: bfloat16 [8192, 128], P(('grp', 'row')), parts along dimension 0, may hold values from -6 to 6
- token_single: bfloat16 [1024, 768], P(('grp', 'row')), parts along dimension 0, may hold values from -6 to 6
- pair_cond: bfloat16 [1024, 512, 128], P(('grp', 'row'), 'smp'), parts along dimension 0, may hold values from -6 to 6
- atom_to_token: int32 [8192], P(('grp', 'row')), parts along dimension 0, may hold values from 0 to 511, as said below
- window_offsets: int32 [256], P(('grp', 'row')), parts along dimension 0, may hold values from -96 to 0
- atom_mask: int32 [8192], P('grp'), parts along dimension 0, may hold values 0 or 1
- token_mask: int32 [1024], P('grp'), parts along dimension 0, may hold values 0 or 1
- coord_in: float32 [3, 128], replicated, may hold values from -3.5 to 3.5
- atom_gain: float32 [2, 128], replicated, may hold values from 0.1 to 1.9
- atom_qkv: bfloat16 [2, 128, 384], replicated, may hold values from -1 to 1
- atom_proj: bfloat16 [2, 128, 128], replicated, may hold values from -0.5 to 0.5
- gather_in: bfloat16 [128, 768], replicated, may hold values from -0.5 to 0.5
- noise_embed: float32 [768], replicated, may hold values from -6 to 6
- pair_gain: float32 [128], replicated, may hold values from 0.1 to 1.9
- pair_heads: bfloat16 [128, 16], replicated, may hold values from -0.5 to 0.5
- token_gain: float32 [2, 768], replicated, may hold values from 0.1 to 1.9
- token_qkv: bfloat16 [768, 2304], replicated, may hold values from -1 to 1
- token_proj: bfloat16 [768, 768], replicated, may hold values from -0.21875 to 0.21875
- ffn_in: bfloat16 [768, 3072], replicated, may hold values from -0.21875 to 0.21875
- ffn_out: bfloat16 [1536, 768], replicated, may hold values from -0.15625 to 0.15625
- scatter_out: bfloat16 [768, 128], replicated, may hold values from -0.21875 to 0.21875
- out_gain: float32 [128], replicated, may hold values from 0.1 to 1.9
- coord_out: bfloat16 [3, 128], replicated, may hold values from -0.5 to 0.5
Outputs:
- token_out: bfloat16 [8, 512, 768], P(('grp', 'smp'), 'row'), parts along dimension 0
- direction: float32 [8, 3, 4096], P(('grp', 'smp'), None, 'row'), parts along dimension 0
There are 2 independent parts, one for each index of `grp`. A program takes and returns all parts, laid end to end along the dimension named above; an argument that names none is the same for every part. Nothing has to cross between parts.
Inputs may be any that keep to these rules, and one draw needn't show every extreme that they name: `atom_to_token`: never falls along the atoms; atoms k * 1024 to (k + 1) * 1024 - 1 belong to tokens k * 128 to (k + 1) * 128 - 1; some tokens have no atom.
All inputs are finite; a program needn't handle non-finite values.
Results may differ from a plain program's by a relative error of at most 0.013.
Values may be sent and summed in bfloat16 or wider, within the bound.
A program may use at most 128 MiB of HBM per device.

v0:
```python
import jax
import jax.numpy as jnp
from jax import lax
from jax.sharding import PartitionSpec as P

D = 768
HEADS = 16
FF = 1536
CA = 128
AHEADS = 4
WQ = 32
WK = 128
HALO = 96
sigma_data = 16.0
gamma_boost = 0.8
norm_eps = 1e-05
masked_score = -1e30
outside_score = -2e30


def with_halo(block, sides, width):
    for axis, dim in sides:
        count = lax.axis_size(axis)
        forward = [(i, i + 1) for i in range(count - 1)]
        backward = [(target, source) for source, target in forward]
        low = lax.ppermute(
            lax.slice_in_dim(block, block.shape[dim] - width, None, axis=dim), axis, forward
        )
        high = lax.ppermute(lax.slice_in_dim(block, 0, width, axis=dim), axis, backward)
        block = jnp.concatenate([low, block, high], axis=dim)
    return block


def layer_norm(values, norm_gain):
    average = jnp.mean(values, axis=-1, keepdims=True)
    centred = values - average
    variance = jnp.mean(centred * centred, axis=-1, keepdims=True)
    return centred * lax.rsqrt(variance + norm_eps) * norm_gain


def softmax_rows(scores):
    largest = jnp.max(scores, axis=-1, keepdims=True)
    exponent = jnp.exp(scores - largest)
    return exponent / jnp.sum(exponent, axis=-1, keepdims=True)


def pair_bias_of(pair_tile, pair_gain, pair_heads):
    normed = layer_norm(pair_tile.astype(jnp.float32), pair_gain).astype(jnp.bfloat16)
    return jnp.einsum("ijc,ch->hij", normed, pair_heads, preferred_element_type=jnp.float32).astype(
        jnp.bfloat16
    )


def block_spans(extended, block_count, span_blocks):
    tail_shape = extended.shape[1:]
    grouped = extended.reshape((block_count + span_blocks - 1, WQ) + tail_shape)
    pieces = [grouped[shift : shift + block_count] for shift in range(span_blocks)]
    return jnp.stack(pieces, axis=1).reshape((block_count, span_blocks * WQ) + tail_shape)


def window_attend(queries, windows, live, inside, w_out):
    block_count = queries.shape[0] // WQ
    head_size = CA // AHEADS
    span_rows = windows.shape[1]
    query_heads = queries.reshape(block_count, WQ, AHEADS, head_size)
    key_heads = windows[:, :, :CA].reshape(block_count, span_rows, AHEADS, head_size)
    value_heads = windows[:, :, CA:].reshape(block_count, span_rows, AHEADS, head_size)
    scores = jnp.einsum(
        "bqhd,bkhd->bhqk", query_heads, key_heads, preferred_element_type=jnp.float32
    ) / jnp.sqrt(jnp.float32(head_size))
    scores = jnp.where(live[:, None, None, :], scores, masked_score)
    scores = jnp.where(inside[:, None, None, :], scores, outside_score)
    weights = softmax_rows(scores).astype(jnp.bfloat16)
    mixed_heads = jnp.einsum(
        "bhqk,bkhd->bqhd", weights, value_heads, preferred_element_type=jnp.float32
    ).astype(jnp.bfloat16)
    return jnp.dot(
        mixed_heads.reshape(block_count * WQ, CA), w_out, preferred_element_type=jnp.float32
    )


def atom_block(atom_state, norm_gain, w_qkv, w_out, offsets, live_ext):
    row_count = atom_state.shape[0]
    normed = layer_norm(atom_state, norm_gain).astype(jnp.bfloat16)
    widened = with_halo(normed, (("row", 0),), HALO)
    projected = jnp.dot(widened, w_qkv, preferred_element_type=jnp.float32).astype(jnp.bfloat16)
    queries = projected[HALO : HALO + row_count, :CA]
    extended = projected[:, CA:]
    block_count = row_count // WQ
    span_blocks = (2 * HALO + WQ) // WQ
    windows = block_spans(extended, block_count, span_blocks)
    live = block_spans(live_ext, block_count, span_blocks) > 0
    relative = jnp.arange(span_blocks * WQ, dtype=jnp.int32)[None, :]
    first_key = offsets[:, None] + HALO
    inside = (relative >= first_key) & (relative < first_key + WK)
    return atom_state + window_attend(queries, windows, live, inside, w_out)


def per_device(
    positions,
    noise_draw,
    noise_level,
    atom_single,
    token_single,
    pair_cond,
    atom_to_token,
    window_offsets,
    atom_mask,
    token_mask,
    coord_in,
    atom_gain,
    atom_qkv,
    atom_proj,
    gather_in,
    noise_embed,
    pair_gain,
    pair_heads,
    token_gain,
    token_qkv,
    token_proj,
    ffn_in,
    ffn_out,
    scatter_out,
    out_gain,
    coord_out,
):
    row_index = lax.axis_index("row")
    tok_rows = token_single.shape[0]
    atom_rows = atom_single.shape[0]
    head_size = D // HEADS
    biases = lax.all_gather(
        pair_bias_of(pair_cond, pair_gain, pair_heads), "smp", axis=2, tiled=True
    )
    local_token = atom_to_token - row_index * tok_rows
    valid_local = lax.dynamic_slice_in_dim(atom_mask, row_index * atom_rows, atom_rows)
    member = (local_token[None, :] == jnp.arange(tok_rows, dtype=jnp.int32)[:, None]) & (
        valid_local[None, :] > 0
    )
    onehot = member.astype(jnp.bfloat16)
    counts = jnp.maximum(jnp.sum(member.astype(jnp.float32), axis=1), 1.0)
    live_padded = jnp.pad(atom_mask, (HALO, HALO))
    live_ext = lax.dynamic_slice_in_dim(live_padded, row_index * atom_rows, atom_rows + 2 * HALO)
    key_live = token_mask > 0
    coords = positions[0]
    kicks = noise_draw[0]
    level_now = noise_level[0]
    level_hat = (1.0 + gamma_boost) * level_now
    noisy = coords + jnp.sqrt(level_hat * level_hat - level_now * level_now) * kicks
    scaled = noisy / jnp.sqrt(level_hat * level_hat + sigma_data * sigma_data)
    atom_state = atom_single.astype(jnp.float32) + jnp.einsum(
        "ka,kc->ac", scaled, coord_in, precision=lax.Precision.HIGHEST
    )
    atom_state = atom_block(
        atom_state, atom_gain[0], atom_qkv[0], atom_proj[0], window_offsets, live_ext
    )
    lifted = jax.nn.relu(
        jnp.dot(atom_state.astype(jnp.bfloat16), gather_in, preferred_element_type=jnp.float32)
    ).astype(jnp.bfloat16)
    pooled = jnp.dot(onehot, lifted, preferred_element_type=jnp.float32) / counts[:, None]
    token_state = (
        pooled
        + token_single.astype(jnp.float32)
        + jnp.log(level_hat / sigma_data) / 4.0 * noise_embed
    )
    normed = layer_norm(token_state, token_gain[0]).astype(jnp.bfloat16)
    projected = jnp.dot(normed, token_qkv, preferred_element_type=jnp.float32).astype(jnp.bfloat16)
    gathered = lax.all_gather(projected[:, D:], "row", axis=0, tiled=True)
    key_count = gathered.shape[0]
    query_heads = projected[:, :D].reshape(tok_rows, HEADS, head_size)
    key_heads = gathered[:, :D].reshape(key_count, HEADS, head_size)
    value_heads = gathered[:, D:].reshape(key_count, HEADS, head_size)
    scores = jnp.einsum(
        "ihd,jhd->hij", query_heads, key_heads, preferred_element_type=jnp.float32
    ) / jnp.sqrt(jnp.float32(head_size))
    scores = scores + biases.astype(jnp.float32)
    scores = jnp.where(key_live[None, None, :], scores, masked_score)
    weights = softmax_rows(scores).astype(jnp.bfloat16)
    mixed_heads = (
        jnp.einsum("hij,jhd->ihd", weights, value_heads, preferred_element_type=jnp.float32)
        .astype(jnp.bfloat16)
        .reshape(tok_rows, D)
    )
    token_state = token_state + jnp.dot(mixed_heads, token_proj, preferred_element_type=jnp.float32)
    normed = layer_norm(token_state, token_gain[1]).astype(jnp.bfloat16)
    hidden = jnp.dot(normed, ffn_in, preferred_element_type=jnp.float32)
    active = (jax.nn.silu(hidden[:, :FF]) * hidden[:, FF:]).astype(jnp.bfloat16)
    token_state = token_state + jnp.dot(active, ffn_out, preferred_element_type=jnp.float32)
    token_result = token_state.astype(jnp.bfloat16)
    spread_back = jnp.dot(token_result, scatter_out, preferred_element_type=jnp.float32).astype(
        jnp.bfloat16
    )
    atom_state = atom_state + lax.dot_general(
        onehot, spread_back, (((0,), (0,)), ((), ())), preferred_element_type=jnp.float32
    )
    atom_state = atom_block(
        atom_state, atom_gain[1], atom_qkv[1], atom_proj[1], window_offsets, live_ext
    )
    normed_out = layer_norm(atom_state, out_gain).astype(jnp.bfloat16)
    update = lax.dot_general(
        coord_out, normed_out, (((1,), (1,)), ((), ())), preferred_element_type=jnp.float32
    )
    base_square = sigma_data * sigma_data + level_hat * level_hat
    skip_scale = sigma_data * sigma_data / base_square
    out_scale = level_hat * sigma_data / jnp.sqrt(base_square)
    denoised = skip_scale * noisy + out_scale * update
    direction = (noisy - denoised) / level_hat
    return (token_result[None], direction[None])


def solution(mesh):
    in_specs = (
        P(("grp", "smp"), None, "row"),
        P(("grp", "smp"), None, "row"),
        P(("grp", "smp")),
        P(("grp", "row"), None),
        P(("grp", "row"), None),
        P(("grp", "row"), "smp", None),
        P(("grp", "row")),
        P(("grp", "row")),
        P("grp"),
        P("grp"),
        P(),
        P(),
        P(),
        P(),
        P(),
        P(),
        P(),
        P(),
        P(),
        P(),
        P(),
        P(),
        P(),
        P(),
        P(),
        P(),
    )
    out_specs = (P(("grp", "smp"), "row", None), P(("grp", "smp"), None, "row"))
    return jax.shard_map(
        per_device, mesh=mesh, in_specs=in_specs, out_specs=out_specs, check_vma=False
    )
```

profile of v0, /device:TPU:0, one launch (start us, length us, event | category | flops | bytes accessed | tf_op | source)
XLA Modules:
  0.0 203.9 jit_solution(14690072002025671553)
XLA Ops:
  8.1 2.2 %fusion.123 = (f32[1024]{0:T(1024)S(1)}, f32[1024,128]{1,0:T(8,128)S(1)}) fusion(f32[3,128]{1,0:T(4,128)} %param.36, f32[]{:T(128)S(6)} %sqrt.8, f32[1,3,1024]{2,0,1:T(1,128)} %param.27, f32[]{:T(128)S(6)} %sqrt.7, f32[1,3,1024]{2,0,1:T(1,128)} %param.26, bf16[1024,128]{1,0:T(8,128)(2,1)} %param.29), kind=kOutput, calls=%fused_computation.202 | convolution fusion | flops 5120000 | bytes 816648 | tf_op jit(solution)/shard_map/ka,kc->ac/dot_general | solution.py:150
  10.7 1.3 slice_bitcast_fusion
  12.4 0.7 copy-done.10
  13.7 5.6 %collective-permute-start = (bf16[96,128]{1,0:T(8,128)(2,1)}, bf16[96,128]{1,0:T(8,128)(2,1)}, u32[]{:S(2)}, u32[]{:S(2)}) collective-permute-start(bf16[96,128]{1,0:T(8,128)(2,1)} %get-tuple-element.32), channel_id=1, source_target_pairs={{0,1},{1,2},{2,3},{4,5},{5,6},{6,7},{8,9},{9,10},{10,11},{12,13},{... | collective-permute-start | bytes 73736 | tf_op jit(solution)/shard_map/ppermute | solution.py:26
  19.3 1.3 collective-permute-start.1
  20.6 1.7 pad_dynamic-slice_fusion.6
  22.2 0.8 stack.88
  23.0 1.4 stack.89
  24.4 1.4 stack.90
  25.7 1.4 stack.91
  27.1 1.4 stack.92
  28.5 1.4 stack.93
  29.8 1.4 stack.94
  31.2 1.6 stack.95
  32.8 1.5 broadcast_compare_fusion
  34.3 0.7 broadcast_add_fusion.1
  35.0 0.7 dynamic-slice_compare_fusion
  35.7 0.7 broadcast_subtract_fusion
  37.1 0.7 fusion.94
  37.8 1.3 broadcast_multiply_fusion.1
  39.1 0.8 slice_reduce_fusion
  39.9 1.5 gt.27
  41.4 1.4 convolution_convert_fusion.2
  43.0 0.7 slice.290
  44.1 2.5 %fusion.117 = (bf16[32,224,128]{2,1,0:T(8,128)(2,1)}, bf16[32,224,128]{2,1,0:T(8,128)(2,1)}) fusion(bf16[32,224,256]{2,1,0:T(8,128)(2,1)S(1)} %bitcast.141), kind=kLoop, calls=%fused_computation.196 | loop fusion | bytes 7340032 | tf_op jit(solution)/shard_map/slice | solution.py:66
  46.5 4.0 %copy.78 = bf16[32,224,128]{1,2,0:T(8,128)(2,1)} copy(bf16[32,224,128]{2,1,0:T(8,128)(2,1)} %get-tuple-element.12) | data formatting | bytes 3670016 | tf_op jit(solution)/shard_map/slice | solution.py:66
  50.5 2.7 %reshape.297 = bf16[32,32,4,32]{3,2,1,0:T(4,128)(2,1)} reshape(bf16[1024,128]{1,0:T(8,128)(2,1)} %slice.290) | data formatting | bytes 524288 | tf_op jit(solution)/shard_map/reshape | solution.py:65
  53.3 3.9 %copy.77 = bf16[32,224,128]{1,2,0:T(8,128)(2,1)} copy(bf16[32,224,128]{2,1,0:T(8,128)(2,1)} %get-tuple-element.13) | data formatting | bytes 3670016 | tf_op jit(solution)/shard_map/slice | solution.py:67
  57.2 2.6 %fusion.49 = f32[32,4,32,224]{3,2,1,0:T(8,128)S(1)} fusion(bf16[32,224,4,32]{1,3,2,0:T(8,128)(2,1)} %bitcast.139, bf16[32,32,4,32]{3,2,1,0:T(4,128)(2,1)} %reshape.297), kind=kOutput, calls=%fused_computation.72 | convolution fusion | flops 58720256 | bytes 5767168 | tf_op jit(solution)/shard_map/bqhd,bkhd->bhqk/dot_general | solution.py:68
  59.9 6.4 %fusion.124 = (f32[32,4,32]{2,1,0:T(4,128)S(1)}, f32[32,4,32,224]{3,2,1,0:T(8,128)S(1)}) fusion(f32[32,4,32,224]{3,2,1,0:T(8,128)S(1)} %fusion.49, pred[32,224]{1,0:T(8,128)(4,1)S(1)} %copy-done.17, pred[32,224]{1,0:T(8,128)(4,1)S(1)} %copy-done.19), kind=kOutput, calls=%fused_computation.203 | output fusion | flops 7340255 | bytes 7370752 | tf_op jit(solution)/shard_map/sub | solution.py:43
  66.3 1.0 fusion.35
  67.3 1.7 copy.80
  69.0 2.9 %reshape.299 = bf16[1024,128]{0,1:T(8,128)(2,1)} reshape(bf16[32,32,4,32]{1,0,3,2:T(8,128)(2,1)} %copy.80) | data formatting | bytes 524288 | tf_op jit(solution)/shard_map/reshape | solution.py:78
  71.9 2.2 %convolution_add_fusion.2 = f32[1024,128]{1,0:T(8,128)} fusion(f32[1024,128]{1,0:T(8,128)} %copy-done.3, bf16[1024,128]{0,1:T(8,128)(2,1)} %reshape.299, bf16[2,128,128]{2,1,0:T(8,128)(2,1)} %param.39), kind=kOutput, calls=%fused_computation.53 | convolution fusion | flops 33685504 | bytes 1343488 | tf_op jit(solution)/shard_map/dot_general | solution.py:77
  74.1 3.3 %fusion.125 = (f32[128]{0:T(128)}, f32[128,768]{1,0:T(8,128)}) fusion(f32[768]{0:T(1024)} %broadcast_multiply_fusion.1, bf16[128,768]{1,0:T(8,128)(2,1)} %param.30, f32[128]{0:T(128)} %broadcast_maximum_fusion, bf16[128,768]{1,0:T(8,128)(2,1)} %param.40, f32[1024,128]{1,0:T(8,128)} %convolution_add_fusion.2, s32[1024]{0:T(1024)S(1)} %broadcast_subtract_fusion, ...), kind=kOutput, calls=%fused_computation.204 | convolution fusion | flops 405110656 | bytes 1319936 | tf_op jit(solution)/shard_map/dot_general | solution.py:159
  77.5 0.7 broadcast_multiply_fusion.6
  78.1 1.2 multiply_reduce_fusion.4
  79.3 1.7 convolution_convert_fusion
  81.0 0.8 copy-done.7
  81.8 0.8 slice.292
  82.9 3.5 %convert_reduce_fusion = f32[128,128]{1,0:T(8,128)S(1)} fusion(bf16[128,128,128]{2,1,0:T(8,128)(2,1)} %param.31), kind=kLoop, calls=%fused_computation.4 | loop fusion | flops 4177920 | bytes 4259840 | tf_op jit(solution)/shard_map/reduce_sum | solution.py:35
  86.5 4.8 %fusion.5 = f32[128,128]{1,0:T(8,128)S(1)} fusion(bf16[128,128,128]{2,1,0:T(8,128)(2,1)S(1)} %copy-done.2, f32[128,128]{1,0:T(8,128)S(1)} %broadcast_multiply_fusion), kind=kLoop, calls=%fused_computation.7 | loop fusion | flops 8372224 | bytes 4325376 | tf_op jit(solution)/shard_map/reduce_sum | solution.py:37
  91.3 5.8 %fusion.8 = bf16[128,128,16]{1,2,0:T(8,128)(2,1)S(1)} fusion(bf16[128,128,128]{2,1,0:T(8,128)(2,1)S(1)} %copy-done.2, f32[128]{0:T(128)S(1)} %copy-done.27, f32[128,128]{1,0:T(8,128)S(1)} %add_rsqrt_fusion, f32[128,128]{1,0:T(8,128)S(1)} %broadcast_multiply_fusion, bf16[128,16]{0,1:T(8,128)(2,1)S(1)} %copy-done.25), kind=kOutput, calls=%fused_computation.10 | convolution fusion | flops 77594624 | bytes 4854272 | tf_op jit(solution)/shard_map/ijc,ch->hij/dot_general | solution.py:49
  97.2 1.0 copy.124
  98.4 23.7 %all-gather.3.cloned.1.call-done = bf16[512,1536]{1,0:T(8,128)(2,1)} async-done(((bf16[128,1536]{1,0:T(8,128)(2,1)}), bf16[512,1536]{1,0:T(8,128)(2,1)}) %all-gather.3.cloned.1.call-update) | async-done | bytes 1572880 | tf_op jit(solution)/shard_map/all_gather | solution.py:167
  122.1 1.5 fusion.118
  124.1 21.2 %all-gather.5.cloned.1.call-done = bf16[16,128,512]{2,1,0:T(8,128)(2,1)} async-done(((bf16[16,128,128]{2,1,0:T(8,128)(2,1)}), bf16[16,128,512]{2,1,0:T(8,128)(2,1)}) %all-gather.5.cloned.1.call-update) | async-done | bytes 2097168 | tf_op jit(solution)/shard_map/all_gather | solution.py:131
  145.4 3.3 %fusion.128 = f32[16,128]{1,0:T(8,128)S(1)} fusion(bf16[16,128,512]{2,1,0:T(8,128)(2,1)} %all-gather.5.cloned.1.call-done, pred[512]{0:T(512)(128)(4,1)S(1)} %broadcast_compare_fusion.1, bf16[128,16,48]{0,2,1:T(8,128)(2,1)S(1)} %bitcast.165, bf16[512,16,48]{0,2,1:T(8,128)(2,1)S(1)} %bitcast.160), kind=kOutput, calls=%fused_computation.205 | convolution fusion | flops 106955264 | bytes 3088896 | tf_op jit(solution)/shard_map/sub | solution.py:43
  148.8 4.5 %fusion.40 = bf16[16,48,128]{2,1,0:T(8,128)(2,1)} fusion(bf16[512,16,48]{0,2,1:T(8,128)(2,1)S(1)} %bitcast.162, f32[16,128]{1,0:T(8,128)S(1)} %fusion.128, bf16[16,128,512]{2,1,0:T(8,128)(2,1)} %all-gather.5.cloned.1.call-done, pred[512]{0:T(512)(128)(4,1)} %copy-done.23, bf16[128,16,48]{0,2,1:T(8,128)(2,1)} %bitcast.166, bf16[512,16,48]{0,2,1:T(8,128)(2,1)S(1)} %bitcast.161), kind=kOutput, calls=%fused_computation.60 | convolution fusion | flops 208767488 | bytes 4071936 | tf_op jit(solution)/shard_map/hij,jhd->ihd/dot_general | solution.py:179
  153.3 1.4 fusion.129
  154.9 3.3 %fusion.79 = f32[128,3072]{1,0:T(8,128)S(1)} fusion(bf16[768,3072]{1,0:T(8,128)(2,1)} %param.47, f32[128,768]{1,0:T(8,128)S(1)} %get-tuple-element.52, f32[768]{0:T(1024)S(1)} %get-tuple-element.8, f32[128]{0:T(128)S(1)} %add_rsqrt_fusion.4, f32[128]{0:T(128)S(1)} %broadcast_multiply_fusion.5), kind=kOutput, calls=%fused_computation.110 | convolution fusion | flops 604372992 | bytes 6688768 | tf_op jit(solution)/shard_map/dot_general | solution.py:185
  160.6 3.4 %collective-permute-start.2 = (bf16[96,128]{1,0:T(8,128)(2,1)S(1)}, bf16[96,128]{1,0:T(8,128)(2,1)S(1)}, u32[]{:S(2)}, u32[]{:S(2)}) collective-permute-start(bf16[96,128]{1,0:T(8,128)(2,1)S(1)} %get-tuple-element.30), channel_id=1, source_target_pairs={{0,1},{1,2},{2,3},{4,5},{5,6},{6,7},{8,9},{9,10},{10,11},{12,13},{... | collective-permute-start | bytes 73736 | tf_op jit(solution)/shard_map/ppermute | solution.py:26
  164.0 1.5 collective-permute-start.3
  165.6 4.1 %collective-permute-done.3 = bf16[96,128]{1,0:T(8,128)(2,1)S(1)} collective-permute-done((bf16[96,128]{1,0:T(8,128)(2,1)S(1)}, bf16[96,128]{1,0:T(8,128)(2,1)S(1)}, u32[]{:S(2)}, u32[]{:S(2)}) %collective-permute-start.3) | collective-permute-done | bytes 24608 | tf_op jit(solution)/shard_map/ppermute | solution.py:29
  170.7 2.5 %fusion.116 = (bf16[32,224,128]{2,1,0:T(8,128)(2,1)}, bf16[32,224,128]{2,1,0:T(8,128)(2,1)}) fusion(bf16[32,224,256]{2,1,0:T(8,128)(2,1)S(1)} %bitcast.142), kind=kLoop, calls=%fused_computation.195 | loop fusion | bytes 7340032 | tf_op jit(solution)/shard_map/slice | solution.py:66
  173.2 3.2 %copy.93 = bf16[32,224,128]{1,2,0:T(8,128)(2,1)S(1)} copy(bf16[32,224,128]{2,1,0:T(8,128)(2,1)} %get-tuple-element.10) | data formatting | bytes 3670016 | tf_op jit(solution)/shard_map/slice | solution.py:66
  176.8 0.7 fusion.47
  177.5 4.3 %fusion.131 = (f32[32,4,32]{2,1,0:T(4,128)}, f32[32,4,32,224]{3,2,1,0:T(8,128)}) fusion(f32[32,4,32,224]{3,2,1,0:T(8,128)S(1)} %fusion.47, pred[32,224]{1,0:T(8,128)(4,1)S(1)} %copy-done.18, pred[32,224]{1,0:T(8,128)(4,1)S(1)} %copy-done.20), kind=kOutput, calls=%fused_computation.208 | output fusion | flops 7340255 | bytes 7370752 | tf_op jit(solution)/shard_map/sub | solution.py:43
  181.8 3.1 %copy.92 = bf16[32,224,128]{1,2,0:T(8,128)(2,1)} copy(bf16[32,224,128]{2,1,0:T(8,128)(2,1)S(1)} %copy-done.5) | data formatting | bytes 3670016 | tf_op jit(solution)/shard_map/slice | solution.py:67
  184.9 3.8 %fusion.36 = bf16[32,32,4,32]{1,3,2,0:T(8,128)(2,1)S(1)} fusion(bf16[32,224,4,32]{1,3,2,0:T(8,128)(2,1)} %bitcast.159, f32[32,4,32,224]{3,2,1,0:T(8,128)} %get-tuple-element.56, f32[32,4,32]{2,1,0:T(4,128)} %get-tuple-element.55), kind=kOutput, calls=%fused_computation.50 | convolution fusion | flops 60686336 | bytes 5783552 | tf_op jit(solution)/shard_map/bhqk,bkhd->bqhd/dot_general | solution.py:74
  188.7 1.7 copy.95
  190.4 2.9 %reshape.308 = bf16[1024,128]{0,1:T(8,128)(2,1)} reshape(bf16[32,32,4,32]{1,0,3,2:T(8,128)(2,1)} %copy.95) | data formatting | bytes 524288 | tf_op jit(solution)/shard_map/reshape | solution.py:78
  193.3 1.6 fusion.132
  195.3 1.2 fusion.46
  (110 shorter events, 8.6 us)
Async XLA Ops:
  7.2 72.2 %copy-start = (bf16[768,2304]{1,0:T(8,128)(2,1)S(1)}, bf16[768,2304]{1,0:T(8,128)(2,1)}, u32[]{:S(2)}) copy-start(bf16[768,2304]{1,0:T(8,128)(2,1)} %param.45) | copy-start | bytes 10616836
  7.2 114.9 %all-gather.3.cloned.1.call-start = ((), (), s32[]{:S(2)}) async-start(), calls=%async_computation | async-start | bytes 1966080 | tf_op jit(solution)/shard_map/all_gather | solution.py:167
  10.3 1.7 copy-start.3
  12.4 0.7 copy-start.10
  13.7 27.7 %collective-permute-start = (bf16[96,128]{1,0:T(8,128)(2,1)}, bf16[96,128]{1,0:T(8,128)(2,1)}, u32[]{:S(2)}, u32[]{:S(2)}) collective-permute-start(bf16[96,128]{1,0:T(8,128)(2,1)} %get-tuple-element.32), channel_id=1, source_target_pairs={{0,1},{1,2},{2,3},{4,5},{5,6},{6,7},{8,9},{9,10},{10,11},{12,13},{... | collective-permute-start | bytes 73736 | tf_op jit(solution)/shard_map/ppermute | solution.py:26
  19.3 22.1 %collective-permute-start.1 = (bf16[96,128]{1,0:T(8,128)(2,1)}, bf16[96,128]{1,0:T(8,128)(2,1)}, u32[]{:S(2)}, u32[]{:S(2)}) collective-permute-start(bf16[96,128]{1,0:T(8,128)(2,1)} %get-tuple-element.33), channel_id=1, source_target_pairs={{1,0},{2,1},{3,2},{5,4},{6,5},{7,6},{9,8},{10,9},{11,10},{13,12},{... | collective-permute-start | bytes 73736 | tf_op jit(solution)/shard_map/ppermute | solution.py:29
  57.2 2.6 %copy-start.17 = (pred[32,224]{1,0:T(8,128)(4,1)S(1)}, pred[32,224]{1,0:T(8,128)(4,1)}, u32[]{:S(2)}) copy-start(pred[32,224]{1,0:T(8,128)(4,1)} %gt.27) | copy-start | bytes 21508
  57.2 2.6 %copy-start.19 = (pred[32,224]{1,0:T(8,128)(4,1)S(1)}, pred[32,224]{1,0:T(8,128)(4,1)}, u32[]{:S(2)}) copy-start(pred[32,224]{1,0:T(8,128)(4,1)} %fusion.94) | copy-start | bytes 21508
  59.9 6.4 %copy-start.8 = (bf16[32,224,128]{1,2,0:T(8,128)(2,1)S(1)}, bf16[32,224,128]{1,2,0:T(8,128)(2,1)}, u32[]{:S(2)}) copy-start(bf16[32,224,128]{1,2,0:T(8,128)(2,1)} %copy.77) | copy-start | bytes 5505028
  81.0 0.8 copy-start.7
  82.7 8.6 %copy-start.25 = (bf16[128,16]{0,1:T(8,128)(2,1)S(1)}, bf16[128,16]{0,1:T(8,128)(2,1)}, u32[]{:S(2)}) copy-start(bf16[128,16]{0,1:T(8,128)(2,1)} %param.43) | copy-start | bytes 12292
  82.7 8.6 %copy-start.27 = (f32[128]{0:T(128)S(1)}, f32[128]{0:T(128)}, u32[]{:S(2)}) copy-start(f32[128]{0:T(128)} %param.42) | copy-start | bytes 1540
  82.7 62.7 %all-gather.5.cloned.1.call-start = ((), (), s32[]{:S(2)}) async-start(), calls=%async_computation.1 | async-start | bytes 2621440 | tf_op jit(solution)/shard_map/all_gather | solution.py:131
  82.9 3.5 %copy-start.2 = (bf16[128,128,128]{2,1,0:T(8,128)(2,1)S(1)}, bf16[128,128,128]{2,1,0:T(8,128)(2,1)}, u32[]{:S(2)}) copy-start(bf16[128,128,128]{2,1,0:T(8,128)(2,1)} %param.31) | copy-start | bytes 12582916
  91.3 6.9 %copy-start.21 = (s32[512]{0:T(512)S(1)}, s32[512]{0:T(512)}, u32[]{:S(2)}) copy-start(s32[512]{0:T(512)} %param.35) | copy-start | bytes 6148
  91.3 6.9 %slice-start = ((bf16[128,2304]{1,0:T(8,128)(2,1)}), bf16[128,768]{1,0:T(8,128)(2,1)S(1)}, s32[]{:S(2)}) async-start(bf16[128,2304]{1,0:T(8,128)(2,1)} %copy-done.7), calls=%async_computation.2 | async-start | bytes 393216 | tf_op jit(solution)/shard_map/slice | solution.py:169
  98.2 50.6 %copy-start.23 = (pred[512]{0:T(512)(128)(4,1)}, pred[512]{0:T(512)(128)(4,1)S(1)}, u32[]{:S(2)}) copy-start(pred[512]{0:T(512)(128)(4,1)S(1)} %broadcast_compare_fusion.1) | copy-start | bytes 1540
  98.3 50.4 %copy-start.14 = (bf16[128,768]{0,1:T(8,128)(2,1)}, bf16[128,768]{0,1:T(8,128)(2,1)S(1)}, u32[]{:S(2)}) copy-start(bf16[128,768]{0,1:T(8,128)(2,1)S(1)} %copy.82) | copy-start | bytes 589828
  148.7 4.5 %copy-start.6 = (f32[128,768]{1,0:T(8,128)S(1)}, f32[128,768]{1,0:T(8,128)}, u32[]{:S(2)}) copy-start(f32[128,768]{1,0:T(8,128)} %get-tuple-element.50) | copy-start | bytes 1179652
  148.8 4.5 %copy-start.11 = (bf16[768,768]{1,0:T(8,128)(2,1)S(1)}, bf16[768,768]{1,0:T(8,128)(2,1)}, u32[]{:S(2)}) copy-start(bf16[768,768]{1,0:T(8,128)(2,1)} %param.46) | copy-start | bytes 3538948
  154.6 3.5 %copy-start.24 = (bf16[1536,768]{1,0:T(8,128)(2,1)S(1)}, bf16[1536,768]{1,0:T(8,128)(2,1)}, u32[]{:S(2)}) copy-start(bf16[1536,768]{1,0:T(8,128)(2,1)} %param.48) | copy-start | bytes 7077892
  158.2 1.0 copy-start.9
  158.2 1.1 copy-start.12
  158.2 2.0 copy-start.22
  158.2 11.5 %copy-start.15 = (bf16[2,128,384]{2,1,0:T(8,128)(2,1)S(1)}, bf16[2,128,384]{2,1,0:T(8,128)(2,1)}, u32[]{:S(2)}) copy-start(bf16[2,128,384]{2,1,0:T(8,128)(2,1)} %param.38) | copy-start | bytes 589828
  159.3 10.8 %copy-start.13 = (bf16[128,768]{1,0:T(8,128)(2,1)}, bf16[128,768]{1,0:T(8,128)(2,1)S(1)}, u32[]{:S(2)}) copy-start(bf16[128,768]{1,0:T(8,128)(2,1)S(1)} %fusion.41) | copy-start | bytes 589828
  159.8 5.8 %copy-start.4 = (f32[1024,128]{1,0:T(8,128)}, f32[1024,128]{1,0:T(8,128)S(1)}, u32[]{:S(2)}) copy-start(f32[1024,128]{1,0:T(8,128)S(1)} %get-tuple-element.54) | copy-start | bytes 1572868
  160.6 5.0 %collective-permute-start.2 = (bf16[96,128]{1,0:T(8,128)(2,1)S(1)}, bf16[96,128]{1,0:T(8,128)(2,1)S(1)}, u32[]{:S(2)}, u32[]{:S(2)}) collective-permute-start(bf16[96,128]{1,0:T(8,128)(2,1)S(1)} %get-tuple-element.30), channel_id=1, source_target_pairs={{0,1},{1,2},{2,3},{4,5},{5,6},{6,7},{8,9},{9,10},{10,11},{12,13},{... | collective-permute-start | bytes 73736 | tf_op jit(solution)/shard_map/ppermute | solution.py:26
  164.0 5.7 %collective-permute-start.3 = (bf16[96,128]{1,0:T(8,128)(2,1)S(1)}, bf16[96,128]{1,0:T(8,128)(2,1)S(1)}, u32[]{:S(2)}, u32[]{:S(2)}) collective-permute-start(bf16[96,128]{1,0:T(8,128)(2,1)S(1)} %get-tuple-element.31), channel_id=1, source_target_pairs={{1,0},{2,1},{3,2},{5,4},{6,5},{7,6},{9,8},{10,9},{11,10},{13,12},{... | collective-permute-start | bytes 73736 | tf_op jit(solution)/shard_map/ppermute | solution.py:29
  176.8 0.7 copy-start.18
  176.8 0.7 copy-start.20
  177.5 4.3 %copy-start.5 = (bf16[32,224,128]{2,1,0:T(8,128)(2,1)S(1)}, bf16[32,224,128]{2,1,0:T(8,128)(2,1)}, u32[]{:S(2)}) copy-start(bf16[32,224,128]{2,1,0:T(8,128)(2,1)} %get-tuple-element.11) | copy-start | bytes 5505028
  184.9 12.2 %copy-start.1 = (bf16[768,2304]{1,0:T(8,128)(2,1)S(1)}, bf16[768,2304]{1,0:T(8,128)(2,1)}, u32[]{:S(2)}) copy-start(bf16[768,2304]{1,0:T(8,128)(2,1)} %param.45) | copy-start | bytes 10616836
  188.7 6.6 %copy-start.16 = (f32[1,3,1024]{2,0,1:T(1,128)S(1)}, f32[1,3,1024]{2,0,1:T(1,128)}, u32[]{:S(2)}) copy-start(f32[1,3,1024]{2,0,1:T(1,128)} %param.27) | copy-start | bytes 36868
  188.7 6.6 %copy-start.26 = (bf16[3,128]{1,0:T(4,128)(2,1)S(1)}, bf16[3,128]{1,0:T(4,128)(2,1)}, u32[]{:S(2)}) copy-start(bf16[3,128]{1,0:T(4,128)(2,1)} %param.51) | copy-start | bytes 2308
Sparse Core Ops, SparseCore 0:
  82.8 39.2 all-gather.2
  123.7 21.6 all-gather.4
where the time goes:
time: 205 us; the launch traced here: 204 us
  local copies, waits for them, and re-layouts  56.3 us (27%)
  waiting for transfers between devices  49.1 us (24%)
  matrix products  41.6 us (20%)
  other arithmetic  29 us (14%)
  between operations  15.9 us (8%)
  starting transfers between devices  12 us (6%)
    all_gather x1, waiting for transfers between devices, per_device(): gathered = lax.all_gather(projected[:, D:], 'row', axis=0, tiled=True)  23.7 us
    all_gather x1, waiting for transfers between devices, per_device(): lax.all_gather(pair_bias_of(pair_cond, pair_gain, pair_heads), 'smp', axi...  21.2 us
    slice x4, local copies, waits for them, and re-layouts, window_attend(): windows[:, :, :CA].reshape(block_count, span_rows, AHEADS, head_size)  12.1 us
    sub x2, other arithmetic, softmax_rows(): exponent = jnp.exp(scores - largest)  10.7 us
    another operation x10, local copies, waits for them, and re-layouts, block_spans(): jnp.stack(pieces, axis=1)  10.6 us
    ppermute x2, starting transfers between devices, with_halo(): lax.ppermute(lax.slice_in_dim(block, block.shape[dim] - width, None, axis...  8.95 us
    reduce_sum x6, other arithmetic, layer_norm(): variance = jnp.mean(centred * centred, axis=-1, keepdims=True)  7.22 us
    slice x2, local copies, waits for them, and re-layouts, window_attend(): windows[:, :, CA:].reshape(block_count, span_rows, AHEADS, head_size)  7.01 us
  transfers between devices with their start and end apart: 6, of which 3 were waited for; matrix products, arithmetic and copies ran while one was open for 19% of the time, Pallas kernels for 0%

commit v1 on v0

--- a/solution.py
+++ b/solution.py
@@ -16,6 +16,18 @@
 norm_eps = 1e-05
 masked_score = -1e30
 outside_score = -2e30
+
+
+def gather_by_bits(value, axis, dim):
+    ways, here, step = (lax.axis_size(axis), lax.axis_index(axis), value.shape[dim])
+    line, have = (value, 1)
+    while have < ways:
+        line = jnp.concatenate(
+            [line, lax.ppermute(line, axis, [(d, (d - have) % ways) for d in range(ways)])],
+            axis=dim,
+        )
+        have = 2 * have
+    return jnp.roll(line, here * step, axis=dim)
 
 
 def with_halo(block, sides, width):
@@ -164,7 +176,7 @@
     )
     normed = layer_norm(token_state, token_gain[0]).astype(jnp.bfloat16)
     projected = jnp.dot(normed, token_qkv, preferred_element_type=jnp.float32).astype(jnp.bfloat16)
-    gathered = lax.all_gather(projected[:, D:], "row", axis=0, tiled=True)
+    gathered = gather_by_bits(projected[:, D:], "row", 0)
     key_count = gathered.shape[0]
     query_heads = projected[:, :D].reshape(tok_rows, HEADS, head_size)
     key_heads = gathered[:, :D].reshape(key_count, HEADS, head_size)

time: 205 us -> 209 us (1.020)
  waiting for transfers between devices: 49.1 us -> 43.2 us
  local copies, waits for them, and re-layouts: 56.3 us -> 61.3 us
  starting transfers between devices: 12 us -> 15.9 us
    ppermute x0 -> x2, waiting for transfers between devices: none -> 39 us  [gather_by_bits(): lax.ppermute(line, axis, [(d, (d - have) % ways) for d in range(ways)])]
    all_gather x1 -> x0, waiting for transfers between devices: 23.7 us -> none  [per_device(): gathered = lax.all_gather(projected[:, D:], 'row', axis=0, tiled=True)]
    all_gather x1, waiting for transfers between devices: 21.2 us -> 0.02 us  [per_device(): lax.all_gather(pair_bias_of(pair_cond, pair_gain, pair_heads), 'smp', axi...]
    ppermute x0 -> x2, starting transfers between devices: none -> 5.84 us  [gather_by_bits(): lax.ppermute(line, axis, [(d, (d - have) % ways) for d in range(ways)])]
    unnamed x69 -> x75, local copies, waits for them, and re-layouts: 3.11 us -> 6.42 us
  transfers between devices with their start and end apart: 6 -> 7, of which waited for: 3 -> 3; matrix products, arithmetic and copies ran while one was open for 19% -> 40% of each run, Pallas kernels for 0% -> 0%
where the time goes in v1:
time: 209 us; the launch traced here: 208 us
  local copies, waits for them, and re-layouts  61.3 us (29%)
  waiting for transfers between devices  43.2 us (21%)
  matrix products  41.7 us (20%)
  other arithmetic  29.6 us (14%)
  starting transfers between devices  15.9 us (8%)
  between operations  15.8 us (8%)
    ppermute x2, waiting for transfers between devices, gather_by_bits(): lax.ppermute(line, axis, [(d, (d - have) % ways) for d in range(ways)])  39 us
    slice x4, local copies, waits for them, and re-layouts, window_attend(): windows[:, :, :CA].reshape(block_count, span_rows, AHEADS, head_size)  12.2 us
    another operation x10, local copies, waits for them, and re-layouts, block_spans(): jnp.stack(pieces, axis=1)  10.7 us
    sub x2, other arithmetic, softmax_rows(): exponent = jnp.exp(scores - largest)  10.7 us
    reduce_sum x6, other arithmetic, layer_norm(): variance = jnp.mean(centred * centred, axis=-1, keepdims=True)  7.22 us
    ppermute x2, starting transfers between devices, with_halo(): lax.ppermute(lax.slice_in_dim(block, block.shape[dim] - width, None, axis...  7.12 us
    slice x2, local copies, waits for them, and re-layouts, window_attend(): windows[:, :, CA:].reshape(block_count, span_rows, AHEADS, head_size)  7.02 us
    unnamed x75, local copies, waits for them, and re-layouts  6.42 us
  transfers between devices with their start and end apart: 7, of which 3 were waited for; matrix products, arithmetic and copies ran while one was open for 40% of the time, Pallas kernels for 0%

profile of v1, /device:TPU:0, one launch (start us, length us, event | category | flops | bytes accessed | tf_op | source)
XLA Modules:
  0.0 207.5 jit_solution(9405036323727527090)
XLA Ops:
  8.1 2.2 %fusion.123 = (f32[1024]{0:T(1024)S(1)}, f32[1024,128]{1,0:T(8,128)S(1)}) fusion(f32[3,128]{1,0:T(4,128)} %param.36, f32[]{:T(128)S(6)} %sqrt.8, f32[1,3,1024]{2,0,1:T(1,128)} %param.27, f32[]{:T(128)S(6)} %sqrt.7, f32[1,3,1024]{2,0,1:T(1,128)} %param.26, bf16[1024,128]{1,0:T(8,128)(2,1)} %param.29), kind=kOutput, calls=%fused_computation.210 | convolution fusion | flops 5120000 | bytes 816648 | tf_op jit(solution)/shard_map/ka,kc->ac/dot_general | solution.py:162
  10.8 1.3 slice_bitcast_fusion
  13.7 5.6 %collective-permute-start = (bf16[96,128]{1,0:T(8,128)(2,1)}, bf16[96,128]{1,0:T(8,128)(2,1)}, u32[]{:S(2)}, u32[]{:S(2)}) collective-permute-start(bf16[96,128]{1,0:T(8,128)(2,1)} %get-tuple-element.34), channel_id=1, source_target_pairs={{0,1},{1,2},{2,3},{4,5},{5,6},{6,7},{8,9},{9,10},{10,11},{12,13},{... | collective-permute-start | bytes 73736 | tf_op jit(solution)/shard_map/ppermute | solution.py:38
  19.3 1.4 collective-permute-start.1
  20.7 3.4 %convert_reduce_fusion = f32[128,128]{1,0:T(8,128)S(1)} fusion(bf16[128,128,128]{2,1,0:T(8,128)(2,1)} %param.31), kind=kLoop, calls=%fused_computation.4 | loop fusion | flops 4177920 | bytes 4259840 | tf_op jit(solution)/shard_map/reduce_sum | solution.py:47
  24.1 4.8 %fusion.5 = f32[128,128]{1,0:T(8,128)S(1)} fusion(bf16[128,128,128]{2,1,0:T(8,128)(2,1)S(1)} %copy-done.2, f32[128,128]{1,0:T(8,128)S(1)} %broadcast_multiply_fusion), kind=kLoop, calls=%fused_computation.7 | loop fusion | flops 8372224 | bytes 4325376 | tf_op jit(solution)/shard_map/reduce_sum | solution.py:49
  28.9 5.9 %fusion.8 = bf16[128,128,16]{1,2,0:T(8,128)(2,1)S(1)} fusion(bf16[128,128,128]{2,1,0:T(8,128)(2,1)S(1)} %copy-done.2, f32[128]{0:T(128)S(1)} %copy-done.28, f32[128,128]{1,0:T(8,128)S(1)} %add_rsqrt_fusion, f32[128,128]{1,0:T(8,128)S(1)} %broadcast_multiply_fusion, bf16[128,16]{0,1:T(8,128)(2,1)S(1)} %copy-done.26), kind=kOutput, calls=%fused_computation.10 | convolution fusion | flops 77594624 | bytes 4854272 | tf_op jit(solution)/shard_map/ijc,ch->hij/dot_general | solution.py:61
  34.8 1.0 copy.124
  36.5 0.8 stack.88
  37.3 1.4 stack.89
  38.6 1.4 stack.90
  40.0 1.4 stack.91
  41.4 1.4 stack.92
  42.7 1.4 stack.93
  44.1 1.4 stack.94
  45.5 1.7 stack.95
  47.1 1.5 broadcast_compare_fusion
  52.1 1.3 broadcast_multiply_fusion.1
  53.4 0.8 slice_reduce_fusion
  54.2 1.5 gt.27
  55.7 1.4 convolution_convert_fusion.2
  58.4 2.6 %fusion.117 = (bf16[32,224,128]{2,1,0:T(8,128)(2,1)}, bf16[32,224,128]{2,1,0:T(8,128)(2,1)}) fusion(bf16[32,224,256]{2,1,0:T(8,128)(2,1)S(1)} %bitcast.141), kind=kLoop, calls=%fused_computation.204 | loop fusion | bytes 7340032 | tf_op jit(solution)/shard_map/slice | solution.py:78
  60.9 4.0 %copy.78 = bf16[32,224,128]{1,2,0:T(8,128)(2,1)} copy(bf16[32,224,128]{2,1,0:T(8,128)(2,1)} %get-tuple-element.12) | data formatting | bytes 3670016 | tf_op jit(solution)/shard_map/slice | solution.py:78
  64.9 2.8 %reshape.297 = bf16[32,32,4,32]{3,2,1,0:T(4,128)(2,1)} reshape(bf16[1024,128]{1,0:T(8,128)(2,1)} %slice.290) | data formatting | bytes 524288 | tf_op jit(solution)/shard_map/reshape | solution.py:77
  67.7 4.0 %copy.77 = bf16[32,224,128]{1,2,0:T(8,128)(2,1)} copy(bf16[32,224,128]{2,1,0:T(8,128)(2,1)} %get-tuple-element.13) | data formatting | bytes 3670016 | tf_op jit(solution)/shard_map/slice | solution.py:79
  71.6 2.6 %fusion.49 = f32[32,4,32,224]{3,2,1,0:T(8,128)S(1)} fusion(bf16[32,224,4,32]{1,3,2,0:T(8,128)(2,1)} %bitcast.139, bf16[32,32,4,32]{3,2,1,0:T(4,128)(2,1)} %reshape.297), kind=kOutput, calls=%fused_computation.72 | convolution fusion | flops 58720256 | bytes 5767168 | tf_op jit(solution)/shard_map/bqhd,bkhd->bhqk/dot_general | solution.py:80
  74.3 6.4 %fusion.124 = (f32[32,4,32]{2,1,0:T(4,128)S(1)}, f32[32,4,32,224]{3,2,1,0:T(8,128)S(1)}) fusion(f32[32,4,32,224]{3,2,1,0:T(8,128)S(1)} %fusion.49, pred[32,224]{1,0:T(8,128)(4,1)S(1)} %copy-done.20, pred[32,224]{1,0:T(8,128)(4,1)S(1)} %copy-done.22), kind=kOutput, calls=%fused_computation.211 | output fusion | flops 7340255 | bytes 7370752 | tf_op jit(solution)/shard_map/sub | solution.py:55
  80.7 1.0 fusion.35
  81.8 1.7 copy.80
  83.4 2.9 %reshape.299 = bf16[1024,128]{0,1:T(8,128)(2,1)} reshape(bf16[32,32,4,32]{1,0,3,2:T(8,128)(2,1)} %copy.80) | data formatting | bytes 524288 | tf_op jit(solution)/shard_map/reshape | solution.py:90
  86.4 2.2 %convolution_add_fusion.2 = f32[1024,128]{1,0:T(8,128)} fusion(f32[1024,128]{1,0:T(8,128)} %copy-done.3, bf16[1024,128]{0,1:T(8,128)(2,1)} %reshape.299, bf16[2,128,128]{2,1,0:T(8,128)(2,1)} %param.39), kind=kOutput, calls=%fused_computation.53 | convolution fusion | flops 33685504 | bytes 1343488 | tf_op jit(solution)/shard_map/dot_general | solution.py:89
  88.5 3.4 %fusion.125 = (f32[128]{0:T(128)}, f32[128,768]{1,0:T(8,128)}) fusion(f32[768]{0:T(1024)} %broadcast_multiply_fusion.1, bf16[128,768]{1,0:T(8,128)(2,1)} %param.30, f32[128]{0:T(128)} %broadcast_maximum_fusion, bf16[128,768]{1,0:T(8,128)(2,1)} %param.40, f32[1024,128]{1,0:T(8,128)} %convolution_add_fusion.2, s32[1024]{0:T(1024)S(1)} %broadcast_subtract_fusion, ...), kind=kOutput, calls=%fused_computation.212 | convolution fusion | flops 405110656 | bytes 1319936 | tf_op jit(solution)/shard_map/dot_general | solution.py:171
  92.6 1.2 multiply_reduce_fusion.4
  93.8 1.7 convolution_convert_fusion
  95.5 0.8 copy-done.6
  96.3 0.8 fusion.120
  97.1 4.5 %collective-permute-start.2 = (bf16[128,1536]{1,0:T(8,128)(2,1)S(1)}, bf16[128,1536]{1,0:T(8,128)(2,1)S(1)}, u32[]{:S(2)}, u32[]{:S(2)}) collective-permute-start(bf16[128,1536]{1,0:T(8,128)(2,1)S(1)} %get-tuple-element.30), channel_id=1, source_target_pairs={{0,3},{1,0},{2,1},{3,2},{4,7},{5,4},{6,5},{7,6},{8,11},{9,8},{10,9... | collective-permute-start | bytes 1179656 | tf_op jit(solution)/shard_map/ppermute | solution.py:26
  101.6 7.9 %collective-permute-done.2 = bf16[128,1536]{1,0:T(8,128)(2,1)S(1)} collective-permute-done((bf16[128,1536]{1,0:T(8,128)(2,1)S(1)}, bf16[128,1536]{1,0:T(8,128)(2,1)S(1)}, u32[]{:S(2)}, u32[]{:S(2)}) %collective-permute-start.2) | collective-permute-done | bytes 393248 | tf_op jit(solution)/shard_map/ppermute | solution.py:26
  109.5 1.4 collective-permute-start.3
  111.6 0.9 slice.293
  112.5 0.8 copy.82
  113.3 0.8 constant_dynamic-update-slice_fusion.11
  114.1 31.2 %collective-permute-done.3 = bf16[256,1536]{1,0:T(8,128)(2,1)S(1)} collective-permute-done((bf16[256,1536]{1,0:T(8,128)(2,1)S(1)}, bf16[256,1536]{1,0:T(8,128)(2,1)S(1)}, u32[]{:S(2)}, u32[]{:S(2)}) %collective-permute-start.3) | collective-permute-done | bytes 786464 | tf_op jit(solution)/shard_map/ppermute | solution.py:26
  145.2 1.0 constant_dynamic-update-slice_fusion.10
  146.2 0.8 constant_dynamic-update-slice_fusion.9
  147.0 0.8 constant_dynamic-update-slice_fusion.8
  147.8 0.9 constant_dynamic-update-slice_fusion.7
  148.7 1.5 constant_dynamic-slice_fusion
  150.8 3.4 %fusion.128 = f32[16,128]{1,0:T(8,128)S(1)} fusion(bf16[16,128,512]{2,1,0:T(8,128)(2,1)} %all-gather.2.cloned.1.call-done, pred[512]{0:T(512)(128)(4,1)S(1)} %broadcast_compare_fusion.1, bf16[128,16,48]{0,2,1:T(8,128)(2,1)S(1)} %bitcast.165, bf16[512,16,48]{0,2,1:T(8,128)(2,1)S(1)} %bitcast.160), kind=kOutput, calls=%fused_computation.213 | convolution fusion | flops 106955264 | bytes 3088896 | tf_op jit(solution)/shard_map/sub | solution.py:55
  154.2 4.5 %fusion.40 = bf16[16,48,128]{2,1,0:T(8,128)(2,1)} fusion(bf16[512,16,48]{0,2,1:T(8,128)(2,1)S(1)} %bitcast.162, f32[16,128]{1,0:T(8,128)S(1)} %fusion.128, bf16[16,128,512]{2,1,0:T(8,128)(2,1)} %all-gather.2.cloned.1.call-done, pred[512]{0:T(512)(128)(4,1)S(1)} %broadcast_compare_fusion.1, bf16[128,16,48]{0,2,1:T(8,128)(2,1)S(1)} %bitcast.166, ...), kind=kOutput, calls=%fused_computation.60 | convolution fusion | flops 208767488 | bytes 4071936 | tf_op jit(solution)/shard_map/hij,jhd->ihd/dot_general | solution.py:191
  158.7 1.4 fusion.129
  160.3 3.3 %fusion.79 = f32[128,3072]{1,0:T(8,128)S(1)} fusion(bf16[768,3072]{1,0:T(8,128)(2,1)} %param.47, f32[128,768]{1,0:T(8,128)S(1)} %get-tuple-element.54, f32[768]{0:T(1024)S(1)} %get-tuple-element.8, f32[128]{0:T(128)S(1)} %add_rsqrt_fusion.4, f32[128]{0:T(128)S(1)} %broadcast_multiply_fusion.5), kind=kOutput, calls=%fused_computation.111 | convolution fusion | flops 604372992 | bytes 6688768 | tf_op jit(solution)/shard_map/dot_general | solution.py:197
  166.0 1.6 collective-permute-start.4
  167.6 1.5 collective-permute-start.5
  169.2 4.1 %collective-permute-done.5 = bf16[96,128]{1,0:T(8,128)(2,1)S(1)} collective-permute-done((bf16[96,128]{1,0:T(8,128)(2,1)S(1)}, bf16[96,128]{1,0:T(8,128)(2,1)S(1)}, u32[]{:S(2)}, u32[]{:S(2)}) %collective-permute-start.5) | collective-permute-done | bytes 24608 | tf_op jit(solution)/shard_map/ppermute | solution.py:41
  174.3 2.5 %fusion.116 = (bf16[32,224,128]{2,1,0:T(8,128)(2,1)}, bf16[32,224,128]{2,1,0:T(8,128)(2,1)}) fusion(bf16[32,224,256]{2,1,0:T(8,128)(2,1)S(1)} %bitcast.142), kind=kLoop, calls=%fused_computation.203 | loop fusion | bytes 7340032 | tf_op jit(solution)/shard_map/slice | solution.py:78
  176.8 3.2 %copy.93 = bf16[32,224,128]{1,2,0:T(8,128)(2,1)S(1)} copy(bf16[32,224,128]{2,1,0:T(8,128)(2,1)} %get-tuple-element.10) | data formatting | bytes 3670016 | tf_op jit(solution)/shard_map/slice | solution.py:78
  181.2 4.3 %fusion.131 = (f32[32,4,32]{2,1,0:T(4,128)}, f32[32,4,32,224]{3,2,1,0:T(8,128)}) fusion(f32[32,4,32,224]{3,2,1,0:T(8,128)S(1)} %fusion.47, pred[32,224]{1,0:T(8,128)(4,1)S(1)} %copy-done.21, pred[32,224]{1,0:T(8,128)(4,1)S(1)} %copy-done.23), kind=kOutput, calls=%fused_computation.216 | output fusion | flops 7340255 | bytes 7370752 | tf_op jit(solution)/shard_map/sub | solution.py:55
  185.4 3.1 %copy.92 = bf16[32,224,128]{1,2,0:T(8,128)(2,1)} copy(bf16[32,224,128]{2,1,0:T(8,128)(2,1)S(1)} %copy-done.5) | data formatting | bytes 3670016 | tf_op jit(solution)/shard_map/slice | solution.py:79
  188.5 3.8 %fusion.36 = bf16[32,32,4,32]{1,3,2,0:T(8,128)(2,1)S(1)} fusion(bf16[32,224,4,32]{1,3,2,0:T(8,128)(2,1)} %bitcast.159, f32[32,4,32,224]{3,2,1,0:T(8,128)} %get-tuple-element.58, f32[32,4,32]{2,1,0:T(4,128)} %get-tuple-element.57), kind=kOutput, calls=%fused_computation.50 | convolution fusion | flops 60686336 | bytes 5783552 | tf_op jit(solution)/shard_map/bhqk,bkhd->bqhd/dot_general | solution.py:86
  192.3 1.7 copy.95
  194.0 2.9 %reshape.308 = bf16[1024,128]{0,1:T(8,128)(2,1)} reshape(bf16[32,32,4,32]{1,0,3,2:T(8,128)(2,1)} %copy.95) | data formatting | bytes 524288 | tf_op jit(solution)/shard_map/reshape | solution.py:90
  196.9 1.6 fusion.132
  198.9 1.2 fusion.46
  (118 shorter events, 15.1 us)
Async XLA Ops:
  7.2 86.6 %copy-start = (bf16[768,2304]{1,0:T(8,128)(2,1)S(1)}, bf16[768,2304]{1,0:T(8,128)(2,1)}, u32[]{:S(2)}) copy-start(bf16[768,2304]{1,0:T(8,128)(2,1)} %param.45) | copy-start | bytes 10616836
  7.2 143.6 %all-gather.2.cloned.1.call-start = ((), (), s32[]{:S(2)}) async-start(), calls=%async_computation | async-start | bytes 2621440 | tf_op jit(solution)/shard_map/all_gather | solution.py:143
  8.1 15.9 %copy-start.2 = (bf16[128,128,128]{2,1,0:T(8,128)(2,1)S(1)}, bf16[128,128,128]{2,1,0:T(8,128)(2,1)}, u32[]{:S(2)}) copy-start(bf16[128,128,128]{2,1,0:T(8,128)(2,1)} %param.31) | copy-start | bytes 12582916
  10.4 1.7 copy-start.3
  12.4 0.7 copy-start.11
  13.7 42.0 %collective-permute-start = (bf16[96,128]{1,0:T(8,128)(2,1)}, bf16[96,128]{1,0:T(8,128)(2,1)}, u32[]{:S(2)}, u32[]{:S(2)}) collective-permute-start(bf16[96,128]{1,0:T(8,128)(2,1)} %get-tuple-element.34), channel_id=1, source_target_pairs={{0,1},{1,2},{2,3},{4,5},{5,6},{6,7},{8,9},{9,10},{10,11},{12,13},{... | collective-permute-start | bytes 73736 | tf_op jit(solution)/shard_map/ppermute | solution.py:38
  19.3 9.6 %copy-start.26 = (bf16[128,16]{0,1:T(8,128)(2,1)S(1)}, bf16[128,16]{0,1:T(8,128)(2,1)}, u32[]{:S(2)}) copy-start(bf16[128,16]{0,1:T(8,128)(2,1)} %param.43) | copy-start | bytes 12292
  19.3 9.6 %copy-start.28 = (f32[128]{0:T(128)S(1)}, f32[128]{0:T(128)}, u32[]{:S(2)}) copy-start(f32[128]{0:T(128)} %param.42) | copy-start | bytes 1540
  19.3 36.4 %collective-permute-start.1 = (bf16[96,128]{1,0:T(8,128)(2,1)}, bf16[96,128]{1,0:T(8,128)(2,1)}, u32[]{:S(2)}, u32[]{:S(2)}) collective-permute-start(bf16[96,128]{1,0:T(8,128)(2,1)} %get-tuple-element.35), channel_id=1, source_target_pairs={{1,0},{2,1},{3,2},{5,4},{6,5},{7,6},{9,8},{10,9},{11,10},{13,12},{... | collective-permute-start | bytes 73736 | tf_op jit(solution)/shard_map/ppermute | solution.py:41
  28.9 6.9 %copy-start.18 = (s32[4096]{0:T(1024)S(1)}, s32[4096]{0:T(1024)}, u32[]{:S(2)}) copy-start(s32[4096]{0:T(1024)} %param.34) | copy-start | bytes 49156
  71.6 2.6 %copy-start.20 = (pred[32,224]{1,0:T(8,128)(4,1)S(1)}, pred[32,224]{1,0:T(8,128)(4,1)}, u32[]{:S(2)}) copy-start(pred[32,224]{1,0:T(8,128)(4,1)} %gt.27) | copy-start | bytes 21508
  71.6 2.6 %copy-start.22 = (pred[32,224]{1,0:T(8,128)(4,1)S(1)}, pred[32,224]{1,0:T(8,128)(4,1)}, u32[]{:S(2)}) copy-start(pred[32,224]{1,0:T(8,128)(4,1)} %fusion.94) | copy-start | bytes 21508
  74.3 6.4 %copy-start.9 = (bf16[32,224,128]{1,2,0:T(8,128)(2,1)S(1)}, bf16[32,224,128]{1,2,0:T(8,128)(2,1)}, u32[]{:S(2)}) copy-start(bf16[32,224,128]{1,2,0:T(8,128)(2,1)} %copy.77) | copy-start | bytes 5505028
  95.5 0.8 copy-start.6
  97.1 49.1 %copy-start.7 = (bf16[128,2304]{1,0:T(8,128)(2,1)S(1)}, bf16[128,2304]{1,0:T(8,128)(2,1)}, u32[]{:S(2)}) copy-start(bf16[128,2304]{1,0:T(8,128)(2,1)} %copy-done.6) | copy-start | bytes 1769476
  97.1 12.3 %collective-permute-start.2 = (bf16[128,1536]{1,0:T(8,128)(2,1)S(1)}, bf16[128,1536]{1,0:T(8,128)(2,1)S(1)}, u32[]{:S(2)}, u32[]{:S(2)}) collective-permute-start(bf16[128,1536]{1,0:T(8,128)(2,1)S(1)} %get-tuple-element.30), channel_id=1, source_target_pairs={{0,3},{1,0},{2,1},{3,2},{4,7},{5,4},{6,5},{7,6},{8,11},{9,8},{10,9... | collective-permute-start | bytes 1179656 | tf_op jit(solution)/shard_map/ppermute | solution.py:26
  109.5 35.7 %collective-permute-start.3 = (bf16[256,1536]{1,0:T(8,128)(2,1)S(1)}, bf16[256,1536]{1,0:T(8,128)(2,1)S(1)}, u32[]{:S(2)}, u32[]{:S(2)}) collective-permute-start(bf16[256,1536]{1,0:T(8,128)(2,1)S(1)} %pad_maximum_fusion), channel_id=1, source_target_pairs={{0,2},{1,3},{2,0},{3,1},{4,6},{5,7},{6,4},{7,5},{8,10},{9,11},{10,... | collective-permute-start | bytes 2359304 | tf_op jit(solution)/shard_map/ppermute | solution.py:26
  147.8 3.0 %copy-start.15 = (bf16[128,768]{0,1:T(8,128)(2,1)S(1)}, bf16[128,768]{0,1:T(8,128)(2,1)}, u32[]{:S(2)}) copy-start(bf16[128,768]{0,1:T(8,128)(2,1)} %copy.82) | copy-start | bytes 589828
  150.8 3.4 %copy-start.16 = (bf16[128,768]{0,1:T(8,128)(2,1)S(1)}, bf16[128,768]{0,1:T(8,128)(2,1)}, u32[]{:S(2)}) copy-start(bf16[128,768]{0,1:T(8,128)(2,1)} %copy.82) | copy-start | bytes 589828
  154.2 4.5 %copy-start.8 = (f32[128,768]{1,0:T(8,128)S(1)}, f32[128,768]{1,0:T(8,128)}, u32[]{:S(2)}) copy-start(f32[128,768]{1,0:T(8,128)} %get-tuple-element.52) | copy-start | bytes 1179652
  154.2 4.5 %copy-start.12 = (bf16[768,768]{1,0:T(8,128)(2,1)S(1)}, bf16[768,768]{1,0:T(8,128)(2,1)}, u32[]{:S(2)}) copy-start(bf16[768,768]{1,0:T(8,128)(2,1)} %param.46) | copy-start | bytes 3538948
  160.1 3.5 %copy-start.25 = (bf16[1536,768]{1,0:T(8,128)(2,1)S(1)}, bf16[1536,768]{1,0:T(8,128)(2,1)}, u32[]{:S(2)}) copy-start(bf16[1536,768]{1,0:T(8,128)(2,1)} %param.48) | copy-start | bytes 7077892
  163.6 1.0 copy-start.10
  163.6 1.1 copy-start.13
  163.6 2.0 copy-start.24
  163.6 9.7 %copy-start.17 = (bf16[2,128,384]{2,1,0:T(8,128)(2,1)S(1)}, bf16[2,128,384]{2,1,0:T(8,128)(2,1)}, u32[]{:S(2)}) copy-start(bf16[2,128,384]{2,1,0:T(8,128)(2,1)} %param.38) | copy-start | bytes 589828
  164.7 9.0 %copy-start.14 = (bf16[128,768]{1,0:T(8,128)(2,1)}, bf16[128,768]{1,0:T(8,128)(2,1)S(1)}, u32[]{:S(2)}) copy-start(bf16[128,768]{1,0:T(8,128)(2,1)S(1)} %fusion.41) | copy-start | bytes 589828
  165.3 4.0 %copy-start.4 = (f32[1024,128]{1,0:T(8,128)}, f32[1024,128]{1,0:T(8,128)S(1)}, u32[]{:S(2)}) copy-start(f32[1024,128]{1,0:T(8,128)S(1)} %get-tuple-element.56) | copy-start | bytes 1572868
  166.0 3.2 %collective-permute-start.4 = (bf16[96,128]{1,0:T(8,128)(2,1)S(1)}, bf16[96,128]{1,0:T(8,128)(2,1)S(1)}, u32[]{:S(2)}, u32[]{:S(2)}) collective-permute-start(bf16[96,128]{1,0:T(8,128)(2,1)S(1)} %get-tuple-element.32), channel_id=1, source_target_pairs={{0,1},{1,2},{2,3},{4,5},{5,6},{6,7},{8,9},{9,10},{10,11},{12,13},{... | collective-permute-start | bytes 73736 | tf_op jit(solution)/shard_map/ppermute | solution.py:38
  167.6 5.7 %collective-permute-start.5 = (bf16[96,128]{1,0:T(8,128)(2,1)S(1)}, bf16[96,128]{1,0:T(8,128)(2,1)S(1)}, u32[]{:S(2)}, u32[]{:S(2)}) collective-permute-start(bf16[96,128]{1,0:T(8,128)(2,1)S(1)} %get-tuple-element.33), channel_id=1, source_target_pairs={{1,0},{2,1},{3,2},{5,4},{6,5},{7,6},{9,8},{10,9},{11,10},{13,12},{... | collective-permute-start | bytes 73736 | tf_op jit(solution)/shard_map/ppermute | solution.py:41
  180.4 0.7 copy-start.21
  180.4 0.7 copy-start.23
  181.1 4.3 %copy-start.5 = (bf16[32,224,128]{2,1,0:T(8,128)(2,1)S(1)}, bf16[32,224,128]{2,1,0:T(8,128)(2,1)}, u32[]{:S(2)}) copy-start(bf16[32,224,128]{2,1,0:T(8,128)(2,1)} %get-tuple-element.11) | copy-start | bytes 5505028
  188.5 12.2 %copy-start.1 = (bf16[768,2304]{1,0:T(8,128)(2,1)S(1)}, bf16[768,2304]{1,0:T(8,128)(2,1)}, u32[]{:S(2)}) copy-start(bf16[768,2304]{1,0:T(8,128)(2,1)} %param.45) | copy-start | bytes 10616836
  192.3 6.6 %copy-start.19 = (f32[1,3,1024]{2,0,1:T(1,128)S(1)}, f32[1,3,1024]{2,0,1:T(1,128)}, u32[]{:S(2)}) copy-start(f32[1,3,1024]{2,0,1:T(1,128)} %param.27) | copy-start | bytes 36868
  192.3 6.6 %copy-start.27 = (bf16[3,128]{1,0:T(4,128)(2,1)S(1)}, bf16[3,128]{1,0:T(4,128)(2,1)}, u32[]{:S(2)}) copy-start(bf16[3,128]{1,0:T(4,128)(2,1)} %param.51) | copy-start | bytes 2308
Sparse Core Ops, SparseCore 0:
  35.9 25.0 all-gather.1
